TPU v7x, 32 devices: a whole 2x2x4 slice. The times are simulated.
32 devices in a mesh: gy: 4 (over x, core), gx: 4 (over z), probe: 2 (over y).
Axes of the slice: x: 2, y: 2, z: 4, core: 2. Of those that a mesh axis runs over, the one named last changes fastest.
Arguments:
- state: bfloat16 [4, 16, 16, 640], P(None, 'gy', 'gx'), may hold values from -6 to 6
- probe_signs: int32 [4, 4, 16, 16, 640], P('probe', None, 'gy', 'gx'), may hold values from -1 to 1, as said below
- timesteps: int32 [4], replicated, may hold values from 0 to 999
- time_table: float32 [1000, 640], replicated, may hold values from -4 to 4
- gn_gain: float32 [640], replicated, may hold values from 0.5 to 1.5
- gn_shift: float32 [640], replicated, may hold values from -3 to 3
- conv_weight: bfloat16 [9, 640, 640], P(None, 'probe'), may hold values from -0.078125 to 0.078125
- conv_bias: float32 [640], replicated, may hold values from -3 to 3
Outputs:
- next_state: bfloat16 [4, 16, 16, 640], P(None, 'gy', 'gx')
- logp_delta: float32 [4], replicated
Inputs may be any that keep to these rules, and one draw needn't show every extreme that they name: `probe_signs`: every entry is -1 or 1.
All inputs are finite; a program needn't handle non-finite values.
Results may differ from a plain program's by a relative error of at most 0.0034.
Values may be sent and summed in bfloat16 or wider, within the bound.
A program may use at most 64 MiB of HBM per device.

v0:
```python
import jax
import jax.numpy as jnp
from jax import lax
from jax.sharding import PartitionSpec as P

GROUPS = 32


def with_halo(block, sides, width):
    for axis, dim in sides:
        count = lax.axis_size(axis)
        forward = [(i, i + 1) for i in range(count - 1)]
        backward = [(target, source) for source, target in forward]
        low = lax.ppermute(
            lax.slice_in_dim(block, block.shape[dim] - width, None, axis=dim), axis, forward
        )
        high = lax.ppermute(lax.slice_in_dim(block, 0, width, axis=dim), axis, backward)
        block = jnp.concatenate([low, block, high], axis=dim)
    return block


def local_conv(padded, weight, height, width):
    count = padded.shape[0]
    chans = padded.shape[3]
    total = jnp.zeros((count * height * width, weight.shape[2]), jnp.float32)
    for tap in range(9):
        row_off = tap // 3
        col_off = tap % 3
        window = padded[:, row_off : row_off + height, col_off : col_off + width, :].reshape(
            -1, chans
        )
        total = total + jnp.dot(window, weight[tap], preferred_element_type=jnp.float32)
    return total


def body(state, probe_signs, timesteps, time_table, gn_gain, gn_shift, conv_weight, conv_bias):
    batch, tile_h, tile_w, chans = state.shape
    probes_here = probe_signs.shape[0]
    group_width = chans // GROUPS
    count = tile_h * lax.axis_size("gy") * tile_w * lax.axis_size("gx") * group_width
    xf = state.astype(jnp.float32)
    signs = probe_signs.astype(jnp.float32)
    grouped = xf.reshape(batch, tile_h, tile_w, GROUPS, group_width)
    signs_grouped = signs.reshape(probes_here, batch, tile_h, tile_w, GROUPS, group_width)
    sum_x = jnp.sum(grouped, axis=(1, 2, 4))
    sum_xx = jnp.sum(grouped * grouped, axis=(1, 2, 4))
    sum_u = jnp.sum(signs_grouped, axis=(2, 3, 5))
    cross = jnp.sum(signs_grouped * grouped[None], axis=(2, 3, 5))
    sum_x, sum_xx, sum_u, cross = lax.psum((sum_x, sum_xx, sum_u, cross), ("gy", "gx"))
    mean_x = sum_x / count
    centered = grouped - mean_x[:, None, None, :, None]
    sum_cu = cross - mean_x[None] * sum_u
    var_x = sum_xx / count - mean_x * mean_x
    sigma = jnp.sqrt(var_x + 1e-05)[:, None, None, :, None]
    normal = (centered / sigma).reshape(batch, tile_h, tile_w, chans)
    mean_u = (sum_u / count)[:, :, None, None, :, None]
    mean_cu = (sum_cu / count)[:, :, None, None, :, None]
    dnormal = (signs_grouped - mean_u) / sigma[None] - centered[None] * mean_cu / (
        sigma * sigma * sigma
    )[None]
    dnormal = dnormal.reshape(probes_here, batch, tile_h, tile_w, chans)
    onehot = (
        timesteps[:, None] == jnp.arange(time_table.shape[0], dtype=jnp.int32)[None, :]
    ).astype(jnp.float32)
    embed = jnp.dot(onehot, time_table, precision=lax.Precision.HIGHEST)
    pre = normal * gn_gain + gn_shift + embed[:, None, None, :]
    sig = jax.nn.sigmoid(pre)
    hidden = (pre * sig).astype(jnp.bfloat16)
    slope = sig * (1.0 + pre * (1.0 - sig)) * gn_gain
    dhidden = (slope[None] * dnormal).astype(jnp.bfloat16)
    flat_tangents = dhidden.reshape(probes_here * batch, tile_h, tile_w, chans)
    stacked = jnp.concatenate([hidden, flat_tangents], axis=0)
    items = stacked.shape[0]
    padded = with_halo(stacked, (("gy", 1), ("gx", 2)), 1)
    summed = local_conv(
        padded, lax.all_gather(conv_weight, "probe", axis=1, tiled=True), tile_h, tile_w
    )
    conv_out = summed.reshape(items, tile_h, tile_w, chans)
    conv_primal = conv_out[:batch]
    tangent = conv_out[batch:].reshape(probes_here, batch, tile_h, tile_w, chans)
    partial_sum = jnp.sum(signs * tangent, axis=(0, 2, 3, 4))
    velocity = conv_primal + conv_bias
    next_state = (xf + 0.25 * velocity).astype(jnp.bfloat16)
    total = lax.psum(partial_sum, ("gy", "gx", "probe"))
    logp_delta = -0.25 / (probes_here * lax.axis_size("probe")) * total
    return (next_state, logp_delta)


def solution(mesh):
    in_specs = (
        P(None, "gy", "gx", None),
        P("probe", None, "gy", "gx", None),
        P(),
        P(),
        P(),
        P(),
        P(None, "probe", None),
        P(),
    )
    out_specs = (P(None, "gy", "gx", None), P())
    return jax.shard_map(body, mesh=mesh, in_specs=in_specs, out_specs=out_specs, check_vma=False)
```

profile of v0, /device:TPU:0, one launch (start us, length us, event | category | flops | bytes accessed | tf_op | source)
XLA Modules:
  0.0 171.3 jit_solution(16463650138915544691)
XLA Ops:
  9.6 63.3 %all-reduce = (f32[4,32]{1,0:T(4,128)S(1)}, f32[4,32]{1,0:T(4,128)S(1)}, f32[2,4,32]{2,1,0:T(4,128)S(1)}, f32[2,4,32]{2,1,0:T(4,128)S(1)}) all-reduce(f32[4,32]{1,0:T(4,128)S(1)} %reduce_sum.62, f32[4,32]{1,0:T(4,128)S(1)} %reduce_sum.59, f32[2,4,32]{2,1,0:T(4,128)S(1)} %reduce_sum.84, ...), channel_id=1, replica_groups=mesh['gy'=4,'gx'=4,'probe'=2] {'gy','gx'}, use_global_device_ids=true, to_apply=%region_5.0 | all-reduce | flops 768 | bytes 6144 | tf_op jit(solution)/shard_map/psum | solution.py:49
  76.8 3.0 %collective-permute-start = (bf16[12,1,4,640]{3,2,1,0:T(4,128)(2,1)S(1)}, bf16[12,1,4,640]{3,2,1,0:T(4,128)(2,1)S(1)}, u32[]{:S(2)}, u32[]{:S(2)}) collective-permute-start(bf16[12,1,4,640]{3,2,1,0:T(4,128)(2,1)S(1)} %get-tuple-element.25), channel_id=1, source_target_pairs={{0,8},{8,16},{16,24},{1,9},{9,17},{17,25},{2,10},{10,18},{18,26},{... | collective-permute-start | bytes 184328 | tf_op jit(solution)/shard_map/ppermute | solution.py:14
  82.0 2.0 %collective-permute-start.2 = (bf16[12,6,1,640]{3,2,1,0:T(2,128)(2,1)}, bf16[12,6,1,640]{3,2,1,0:T(2,128)(2,1)}, u32[]{:S(2)}, u32[]{:S(2)}) collective-permute-start(bf16[12,6,1,640]{3,2,1,0:T(2,128)(2,1)} %get-tuple-element.20), channel_id=1, source_target_pairs={{0,2},{2,4},{4,6},{1,3},{3,5},{5,7},{8,10},{10,12},{12,14},{9,11},... | collective-permute-start | bytes 276488 | tf_op jit(solution)/shard_map/ppermute | solution.py:14
  86.4 1.7 reshape.83
  89.9 3.4 %collective-permute-done.3 = bf16[12,6,1,640]{3,2,1,0:T(2,128)(2,1)} collective-permute-done((bf16[12,6,1,640]{3,2,1,0:T(2,128)(2,1)}, bf16[12,6,1,640]{3,2,1,0:T(2,128)(2,1)}, u32[]{:S(2)}, u32[]{:S(2)}) %collective-permute-start.3) | collective-permute-done | bytes 92192 | tf_op jit(solution)/shard_map/ppermute | solution.py:17
  93.3 1.7 maximum_maximum_fusion
  95.0 1.6 fusion.7
  96.6 1.7 %reshape.90 = bf16[192,640]{1,0:T(8,128)(2,1)} reshape(bf16[12,4,4,640]{3,2,1,0:T(4,128)(2,1)} %get-tuple-element.34) | data formatting | bytes 491520 | tf_op jit(solution)/shard_map/reshape | solution.py:29
  98.3 1.7 %reshape.82 = bf16[192,640]{1,0:T(8,128)(2,1)} reshape(bf16[12,4,4,640]{3,2,1,0:T(4,128)(2,1)} %get-tuple-element.14) | data formatting | bytes 491520 | tf_op jit(solution)/shard_map/reshape | solution.py:29
  100.0 1.7 reshape.84
  101.7 1.7 reshape.85
  103.4 1.7 %reshape.87 = bf16[192,640]{1,0:T(8,128)(2,1)} reshape(bf16[12,4,4,640]{3,2,1,0:T(4,128)(2,1)} %get-tuple-element.35) | data formatting | bytes 491520 | tf_op jit(solution)/shard_map/reshape | solution.py:29
  105.2 1.7 %reshape.88 = bf16[192,640]{1,0:T(8,128)(2,1)} reshape(bf16[12,4,4,640]{3,2,1,0:T(4,128)(2,1)} %get-tuple-element.12) | data formatting | bytes 491520 | tf_op jit(solution)/shard_map/reshape | solution.py:29
  106.9 1.7 fusion.1
  108.6 1.6 fusion.2
  110.2 1.6 convolution_add_fusion.6
  111.8 1.6 convolution_add_fusion.5
  113.4 1.6 convolution_add_fusion.4
  115.0 1.5 convolution_add_fusion.3
  116.6 1.5 convolution_add_fusion.2
  118.1 1.5 convolution_add_fusion.1
  119.7 1.5 fusion
  123.2 39.2 %psum.39 = f32[4]{0:T(128)S(1)} all-reduce(f32[4]{0:T(128)S(1)} %multiply_reduce_fusion), channel_id=1, replica_groups=mesh['gy'=4,'gx'=4,'probe'=2] {'gy','gx','probe'}, use_global_device_ids=true, to_apply=%region_13.14 | all-reduce | flops 4 | bytes 32 | tf_op jit(solution)/shard_map/psum | solution.py:84
  162.9 1.6 add_convert_fusion
  (74 shorter events, 14.9 us)
Async XLA Ops:
  7.2 66.8 %copy-start = (f32[1000,640]{1,0:T(8,128)S(1)}, f32[1000,640]{1,0:T(8,128)}, u32[]{:S(2)}) copy-start(f32[1000,640]{1,0:T(8,128)} %param.11) | copy-start | bytes 7680004
  7.2 1.0 copy-start.2
  7.2 1.6 copy-start.1
  7.2 66.8 %copy-start.13 = (s32[4]{0:T(128)S(1)}, s32[4]{0:T(128)}, u32[]{:S(2)}) copy-start(s32[4]{0:T(128)} %param.10) | copy-start | bytes 52
  7.2 99.7 %all-gather.2.cloned.1.call-start = ((), (), s32[]{:S(2)}) async-start(), calls=%async_computation | async-start | bytes 11059200 | tf_op jit(solution)/shard_map/all_gather | solution.py:76
  8.2 66.7 %copy-start.10 = (f32[640]{0:T(1024)S(1)}, f32[640]{0:T(1024)}, u32[]{:S(2)}) copy-start(f32[640]{0:T(1024)} %param.13) | copy-start | bytes 7684
  8.2 66.7 %copy-start.11 = (f32[640]{0:T(1024)S(1)}, f32[640]{0:T(1024)}, u32[]{:S(2)}) copy-start(f32[640]{0:T(1024)} %param.12) | copy-start | bytes 7684
  75.5 4.3 %collective-permute-start.1 = (bf16[12,1,4,640]{3,2,1,0:T(4,128)(2,1)S(1)}, bf16[12,1,4,640]{3,2,1,0:T(4,128)(2,1)S(1)}, u32[]{:S(2)}, u32[]{:S(2)}) collective-permute-start(bf16[12,1,4,640]{3,2,1,0:T(4,128)(2,1)S(1)} %get-tuple-element.26), channel_id=1, source_target_pairs={{8,0},{16,8},{24,16},{9,1},{17,9},{25,17},{10,2},{18,10},{26,18},{... | collective-permute-start | bytes 184328 | tf_op jit(solution)/shard_map/ppermute | solution.py:17
  76.8 3.9 %collective-permute-start = (bf16[12,1,4,640]{3,2,1,0:T(4,128)(2,1)S(1)}, bf16[12,1,4,640]{3,2,1,0:T(4,128)(2,1)S(1)}, u32[]{:S(2)}, u32[]{:S(2)}) collective-permute-start(bf16[12,1,4,640]{3,2,1,0:T(4,128)(2,1)S(1)} %get-tuple-element.25), channel_id=1, source_target_pairs={{0,8},{8,16},{16,24},{1,9},{9,17},{17,25},{2,10},{10,18},{18,26},{... | collective-permute-start | bytes 184328 | tf_op jit(solution)/shard_map/ppermute | solution.py:14
  82.0 7.9 %collective-permute-start.2 = (bf16[12,6,1,640]{3,2,1,0:T(2,128)(2,1)}, bf16[12,6,1,640]{3,2,1,0:T(2,128)(2,1)}, u32[]{:S(2)}, u32[]{:S(2)}) collective-permute-start(bf16[12,6,1,640]{3,2,1,0:T(2,128)(2,1)} %get-tuple-element.20), channel_id=1, source_target_pairs={{0,2},{2,4},{4,6},{1,3},{3,5},{5,7},{8,10},{10,12},{12,14},{9,11},... | collective-permute-start | bytes 276488 | tf_op jit(solution)/shard_map/ppermute | solution.py:14
  84.0 9.3 %collective-permute-start.3 = (bf16[12,6,1,640]{3,2,1,0:T(2,128)(2,1)}, bf16[12,6,1,640]{3,2,1,0:T(2,128)(2,1)}, u32[]{:S(2)}, u32[]{:S(2)}) collective-permute-start(bf16[12,6,1,640]{3,2,1,0:T(2,128)(2,1)} %get-tuple-element.21), channel_id=1, source_target_pairs={{2,0},{4,2},{6,4},{3,1},{5,3},{7,5},{10,8},{12,10},{14,12},{11,9},... | collective-permute-start | bytes 276488 | tf_op jit(solution)/shard_map/ppermute | solution.py:17
  96.6 12.1 %copy-start.3 = (bf16[192,640]{1,0:T(8,128)(2,1)S(1)}, bf16[192,640]{1,0:T(8,128)(2,1)}, u32[]{:S(2)}) copy-start(bf16[192,640]{1,0:T(8,128)(2,1)} %reshape.83) | copy-start | bytes 737284
  106.9 3.3 %copy-start.9 = (bf16[192,640]{1,0:T(8,128)(2,1)S(1)}, bf16[192,640]{1,0:T(8,128)(2,1)}, u32[]{:S(2)}) copy-start(bf16[192,640]{1,0:T(8,128)(2,1)} %reshape.82) | copy-start | bytes 737284
  106.9 4.9 %copy-start.8 = (bf16[192,640]{1,0:T(8,128)(2,1)S(1)}, bf16[192,640]{1,0:T(8,128)(2,1)}, u32[]{:S(2)}) copy-start(bf16[192,640]{1,0:T(8,128)(2,1)} %reshape.84) | copy-start | bytes 737284
  108.6 4.8 %copy-start.7 = (bf16[192,640]{1,0:T(8,128)(2,1)S(1)}, bf16[192,640]{1,0:T(8,128)(2,1)}, u32[]{:S(2)}) copy-start(bf16[192,640]{1,0:T(8,128)(2,1)} %reshape.85) | copy-start | bytes 737284
  110.2 4.8 %copy-start.4 = (bf16[192,640]{1,0:T(8,128)(2,1)S(1)}, bf16[192,640]{1,0:T(8,128)(2,1)}, u32[]{:S(2)}) copy-start(bf16[192,640]{1,0:T(8,128)(2,1)} %reshape.86) | copy-start | bytes 737284
  111.8 4.7 %copy-start.5 = (bf16[192,640]{1,0:T(8,128)(2,1)S(1)}, bf16[192,640]{1,0:T(8,128)(2,1)}, u32[]{:S(2)}) copy-start(bf16[192,640]{1,0:T(8,128)(2,1)} %reshape.87) | copy-start | bytes 737284
  113.4 4.7 %copy-start.6 = (bf16[192,640]{1,0:T(8,128)(2,1)S(1)}, bf16[192,640]{1,0:T(8,128)(2,1)}, u32[]{:S(2)}) copy-start(bf16[192,640]{1,0:T(8,128)(2,1)} %reshape.88) | copy-start | bytes 737284
  119.7 43.3 %copy-start.12 = (f32[640]{0:T(1024)S(1)}, f32[640]{0:T(1024)}, u32[]{:S(2)}) copy-start(f32[640]{0:T(1024)} %param.15) | copy-start | bytes 7684
Sparse Core Ops, SparseCore 0:
  9.6 95.2 all-gather.1
where the time goes:
time: 172 us; the launch traced here: 171 us
  blocking collectives  103 us (60%)
  local copies, waits for them, and re-layouts  20 us (12%)
  matrix products  15.1 us (9%)
  between operations  14.5 us (8%)
  starting transfers between devices  7.62 us (4%)
  other arithmetic  6.68 us (4%)
  waiting for transfers between devices  4.95 us (3%)
    psum x1, blocking collectives, body(): lax.psum((sum_x, sum_xx, sum_u, cross), ('gy', 'gx'))  63.3 us
    psum x1, blocking collectives, body(): total = lax.psum(partial_sum, ('gy', 'gx', 'probe'))  39.2 us
    dot_general x9, matrix products, local_conv(): jnp.dot(window, weight[tap], preferred_element_type=jnp.float32)  14.1 us
    reshape x9, local copies, waits for them, and re-layouts, local_conv(): padded[:, row_off:row_off + height, col_off:col_off + width, :]  13.8 us
    ppermute x2, starting transfers between devices, with_halo(): lax.ppermute(lax.slice_in_dim(block, block.shape[dim] - width, None, axis...  5.01 us
  transfers between devices with their start and end apart: 5, of which 2 were waited for; matrix products, arithmetic and copies ran while one was open for 14% of the time, Pallas kernels for 0%

commit v1 on v0

--- a/solution.py
+++ b/solution.py
@@ -33,7 +33,70 @@
     return total
 
 
-def body(state, probe_signs, timesteps, time_table, gn_gain, gn_shift, conv_weight, conv_bias):
+def travelling_probes(state, probe_signs, timesteps, time_table, gn_gain, gn_shift, conv_weight, conv_bias):
+    batch, tile_h, tile_w, chans = state.shape
+    share = conv_weight.shape[1]
+    group_width = chans // GROUPS
+    ny, nx = lax.axis_size("gy"), lax.axis_size("gx")
+    count = tile_h * ny * tile_w * nx * group_width
+    xf = state.astype(jnp.float32)
+    signs = lax.all_gather(probe_signs.astype(jnp.bfloat16), "probe", axis=0, tiled=True)
+    probes = signs.shape[0]
+    first = lax.axis_index("probe") * share
+
+    def mine(array):
+        return lax.dynamic_slice_in_dim(array, first, share, axis=array.ndim - 1)
+
+    stacked = jnp.concatenate([state[None], signs], axis=0)
+    stacked = mine(stacked).reshape((1 + probes) * batch, tile_h, tile_w, share)
+    padded = with_halo(stacked, (("gy", 1), ("gx", 2)), 1)
+    padded = padded.reshape(1 + probes, batch, tile_h + 2, tile_w + 2, share).astype(jnp.float32)
+
+    cells_x = jnp.stack([jnp.sum(xf, axis=(1, 2)), jnp.sum(xf * xf, axis=(1, 2))])
+    signs_f = signs.astype(jnp.float32)
+    cells_u = jnp.stack([jnp.sum(signs_f, axis=(2, 3)), jnp.sum(signs_f * xf[None], axis=(2, 3))])
+    cells = jnp.concatenate([cells_x, cells_u.reshape(2 * probes, batch, chans)], axis=0)
+    sums = jnp.sum(cells.reshape(2 + 2 * probes, batch, GROUPS, group_width), axis=3)
+    sums = lax.psum(sums, ("gy", "gx")) / count
+    mean_x, mean_xx = sums[0], sums[1]
+    mean_u, cross = sums[2 : 2 + probes], sums[2 + probes :]
+    sigma = jnp.sqrt(mean_xx - mean_x * mean_x + 1e-05)
+    mean_cu = cross - mean_x[None] * mean_u
+    inv = 1.0 / sigma
+    table = jnp.concatenate([mean_x[None], inv[None], mean_u, mean_cu * (inv * inv * inv)], axis=0)
+    table = mine(jnp.repeat(table, group_width, axis=2))[:, :, None, None, :]
+
+    onehot = (
+        timesteps[:, None] == jnp.arange(time_table.shape[0], dtype=jnp.int32)[None, :]
+    ).astype(jnp.float32)
+    embed = jnp.dot(onehot, time_table, precision=lax.Precision.HIGHEST)
+    offset = mine(gn_shift + embed)[:, None, None, :]
+    gain = mine(gn_gain)
+    centered = padded[0] - table[0]
+    pre = centered * table[1] * gain + offset
+    sig = jax.nn.sigmoid(pre)
+    rows = lax.axis_index("gy") * tile_h - 1 + jnp.arange(tile_h + 2)
+    cols = lax.axis_index("gx") * tile_w - 1 + jnp.arange(tile_w + 2)
+    inside = ((rows >= 0) & (rows < tile_h * ny))[:, None] & (
+        (cols >= 0) & (cols < tile_w * nx)
+    )[None, :]
+    inside = inside[:, :, None]
+    hidden = jnp.where(inside, pre * sig, 0.0).astype(jnp.bfloat16)
+    slope = jnp.where(inside, sig * (1.0 + pre * (1.0 - sig)) * gain, 0.0)
+    dnormal = (padded[1:] - table[2 : 2 + probes]) * table[1] - centered * table[2 + probes :]
+    dhidden = (slope[None] * dnormal).astype(jnp.bfloat16)
+
+    velocity = local_conv(hidden, conv_weight, tile_h, tile_w)
+    velocity = lax.psum(velocity, "probe").reshape(batch, tile_h, tile_w, chans) + conv_bias
+    next_state = (xf + 0.25 * velocity).astype(jnp.bfloat16)
+    tangent = local_conv(
+        dhidden.reshape(probes * batch, tile_h + 2, tile_w + 2, share), conv_weight, tile_h, tile_w
+    ).reshape(signs.shape)
+    total = lax.psum(jnp.sum(signs_f * tangent, axis=(0, 2, 3, 4)), ("gy", "gx", "probe"))
+    return (next_state, -0.25 / probes * total)
+
+
+def gathered_weights(state, probe_signs, timesteps, time_table, gn_gain, gn_shift, conv_weight, conv_bias):
     batch, tile_h, tile_w, chans = state.shape
     probes_here = probe_signs.shape[0]
     group_width = chans // GROUPS
@@ -87,6 +150,10 @@
 
 
 def solution(mesh):
+    def body(*args):
+        wide = args[6].shape[1] >= 128
+        return (travelling_probes if wide else gathered_weights)(*args)
+
     in_specs = (
         P(None, "gy", "gx", None),
         P("probe", None, "gy", "gx", None),

time: 172 us -> 217 us (1.26)
  local copies, waits for them, and re-layouts: 20 us -> 39.6 us
  other arithmetic: 6.68 us -> 15.3 us
  blocking collectives: 103 us -> 111 us
  matrix products: 15.1 us -> 21.1 us
  starting transfers between devices: 7.62 us -> 10.2 us
    reshape x9 -> x18, local copies, waits for them, and re-layouts: 13.8 us -> 27.3 us  [local_conv(): padded[:, row_off:row_off + height, col_off:col_off + width, :]]
    all_gather x0 -> x1, blocking collectives: none -> 7.85 us  [travelling_probes(): lax.all_gather(probe_signs.astype(jnp.bfloat16), 'probe', axis=0, tiled=T...]
    dot_general x9 -> x18, matrix products: 14.1 us -> 20.2 us  [local_conv(): jnp.dot(window, weight[tap], preferred_element_type=jnp.float32)]
    convert_element_type x4 -> x6, other arithmetic: 1.99 us -> 7.3 us  [the longest x1 1.66 us: travelling_probes(): next_state = (xf + 0.25 * velocity).astype(jnp.bfloat16)]
    reshape x1 -> x3, local copies, waits for them, and re-layouts: 0.09 us -> 4.42 us  [the longest x1 1.63 us: travelling_probes(): lax.psum(velocity, 'probe').reshape(batch, tile_h, tile_w, chans)]
    concatenate x3 -> x1, other arithmetic: 3.15 us -> 0.28 us  [with_halo(): block = jnp.concatenate([low, block, high], axis=dim)]
    ppermute x2, starting transfers between devices: 5.01 us -> 7.59 us  [with_halo(): lax.ppermute(lax.slice_in_dim(block, block.shape[dim] - width, None, axis...]
  transfers between devices with their start and end apart: 5 -> 5, of which waited for: 2 -> 2; matrix products, arithmetic and copies ran while one was open for 14% -> 6% of each run, Pallas kernels for 0% -> 0%
where the time goes in v1:
time: 217 us; the launch traced here: 215 us
  blocking collectives  111 us (51%)
  local copies, waits for them, and re-layouts  39.6 us (18%)
  matrix products  21.1 us (10%)
  other arithmetic  15.3 us (7%)
  between operations  14.5 us (7%)
  starting transfers between devices  10.2 us (5%)
  waiting for transfers between devices  2.96 us (1%)
    psum x1, blocking collectives, travelling_probes(): sums = lax.psum(sums, ('gy', 'gx')) / count  61.5 us
    psum x1, blocking collectives, travelling_probes(): lax.psum(jnp.sum(signs_f * tangent, axis=(0, 2, 3, 4)), ('gy', 'gx', 'pro...  42 us
    reshape x18, local copies, waits for them, and re-layouts, local_conv(): padded[:, row_off:row_off + height, col_off:col_off + width, :]  27.3 us
    dot_general x18, matrix products, local_conv(): jnp.dot(window, weight[tap], preferred_element_type=jnp.float32)  20.2 us
    all_gather x1, blocking collectives, travelling_probes(): lax.all_gather(probe_signs.astype(jnp.bfloat16), 'probe', axis=0, tiled=T...  7.85 us
    ppermute x2, starting transfers between devices, with_halo(): lax.ppermute(lax.slice_in_dim(block, block.shape[dim] - width, None, axis...  7.59 us
  transfers between devices with their start and end apart: 5, of which 2 were waited for; matrix products, arithmetic and copies ran while one was open for 6% of the time, Pallas kernels for 0%

profile of v1, /device:TPU:0, one launch (start us, length us, event | category | flops | bytes accessed | tf_op | source)
XLA Modules:
  0.0 215.1 jit_solution(14110770725235641444)
XLA Ops:
  8.4 7.9 %all_gather.3 = bf16[4,4,4,4,640]{4,3,2,1,0:T(4,128)(2,1)S(1)} all-gather(bf16[2,4,4,4,640]{4,3,2,1,0:T(4,128)(2,1)S(1)} %convert_element_type.24), channel_id=1, replica_groups=mesh['gy'=4,'gx'=4,'probe'=2] {'probe'}, dimensions={0}, use_global_device_ids=true | all-gather | bytes 491520 | tf_op jit(solution)/shard_map/all_gather | solution.py:43
  19.4 3.0 %collective-permute-start = (bf16[20,1,4,320]{3,2,1,0:T(4,128)(2,1)}, bf16[20,1,4,320]{3,2,1,0:T(4,128)(2,1)S(1)}, u32[]{:S(2)}, u32[]{:S(2)}) collective-permute-start(bf16[20,1,4,320]{3,2,1,0:T(4,128)(2,1)} %get-tuple-element.21), channel_id=1, source_target_pairs={{0,8},{8,16},{16,24},{1,9},{9,17},{17,25},{2,10},{10,18},{18,26},{... | collective-permute-start | bytes 153608 | tf_op jit(solution)/shard_map/ppermute | solution.py:14
  28.4 61.5 %psum.21 = f32[10,4,32]{2,1,0:T(4,128)S(1)} all-reduce(f32[10,4,32]{2,1,0:T(4,128)S(1)} %maximum_reduce_fusion), channel_id=1, replica_groups=mesh['gy'=4,'gx'=4,'probe'=2] {'gy','gx'}, use_global_device_ids=true, to_apply=%region_5.0 | all-reduce | flops 1280 | bytes 10240 | tf_op jit(solution)/shard_map/psum | solution.py:60
  91.1 1.5 reshape.118
  97.6 4.6 %collective-permute-start.2 = (bf16[20,6,1,320]{3,2,1,0:T(2,128)(2,1)S(1)}, bf16[20,6,1,320]{3,2,1,0:T(2,128)(2,1)S(1)}, u32[]{:S(2)}, u32[]{:S(2)}) collective-permute-start(bf16[20,6,1,320]{3,2,1,0:T(2,128)(2,1)S(1)} %get-tuple-element.19), channel_id=1, source_target_pairs={{0,2},{2,4},{4,6},{1,3},{3,5},{5,7},{8,10},{10,12},{12,14},{9,11},... | collective-permute-start | bytes 230408 | tf_op jit(solution)/shard_map/ppermute | solution.py:14
  102.3 1.5 collective-permute-done.3
  105.2 1.7 select_bitcast_fusion
  118.7 1.5 reshape.126
  131.6 1.9 convolution_add_fusion.8
  133.5 1.6 reshape.128
  135.1 1.5 fusion.2
  137.8 1.7 fusion.64
  141.8 1.7 reshape.131
  143.4 1.7 reshape.132
  145.1 1.7 reshape.133
  146.8 1.7 reshape.134
  148.5 1.7 reshape.135
  150.2 1.7 reshape.136
  151.9 1.7 reshape.137
  153.6 1.7 reshape.138
  155.3 1.6 convolution_add_fusion.7
  156.9 1.5 convolution_add_fusion.6
  164.0 42.0 %psum.23 = f32[4]{0:T(128)S(1)} all-reduce(f32[4]{0:T(128)S(1)} %fusion.1), channel_id=1, replica_groups=mesh['gy'=4,'gx'=4,'probe'=2] {'gy','gx','probe'}, use_global_device_ids=true, to_apply=%region_8.9 | all-reduce | flops 4 | bytes 32 | tf_op jit(solution)/shard_map/psum | solution.py:95
  206.6 1.7 add_convert_fusion
  (99 shorter events, 50.5 us)
Async XLA Ops:
  7.2 85.5 %copy-start = (f32[1000,640]{1,0:T(8,128)S(1)}, f32[1000,640]{1,0:T(8,128)}, u32[]{:S(2)}) copy-start(f32[1000,640]{1,0:T(8,128)} %param.11) | copy-start | bytes 7680004
  7.2 85.5 %copy-start.16 = (s32[4]{0:T(128)S(1)}, s32[4]{0:T(128)}, u32[]{:S(2)}) copy-start(s32[4]{0:T(128)} %param.10) | copy-start | bytes 52
  7.2 199.4 %all-reduce.2.cloned.1.call-start = ((), (), s32[]{:S(2)}) async-start(), calls=%async_computation | async-start | bytes 327680 | tf_op jit(solution)/shard_map/psum | solution.py:90
  17.4 78.3 %copy-start.15 = (f32[640]{0:T(1024)S(1)}, f32[640]{0:T(1024)}, u32[]{:S(2)}) copy-start(f32[640]{0:T(1024)} %param.12) | copy-start | bytes 7684
  18.1 77.7 %collective-permute-start.1 = (bf16[20,1,4,320]{3,2,1,0:T(4,128)(2,1)}, bf16[20,1,4,320]{3,2,1,0:T(4,128)(2,1)S(1)}, u32[]{:S(2)}, u32[]{:S(2)}) collective-permute-start(bf16[20,1,4,320]{3,2,1,0:T(4,128)(2,1)} %get-tuple-element.22), channel_id=1, source_target_pairs={{8,0},{16,8},{24,16},{9,1},{17,9},{25,17},{10,2},{18,10},{26,18},{... | collective-permute-start | bytes 153608 | tf_op jit(solution)/shard_map/ppermute | solution.py:17
  19.4 76.4 %collective-permute-start = (bf16[20,1,4,320]{3,2,1,0:T(4,128)(2,1)}, bf16[20,1,4,320]{3,2,1,0:T(4,128)(2,1)S(1)}, u32[]{:S(2)}, u32[]{:S(2)}) collective-permute-start(bf16[20,1,4,320]{3,2,1,0:T(4,128)(2,1)} %get-tuple-element.21), channel_id=1, source_target_pairs={{0,8},{8,16},{16,24},{1,9},{9,17},{17,25},{2,10},{10,18},{18,26},{... | collective-permute-start | bytes 153608 | tf_op jit(solution)/shard_map/ppermute | solution.py:14
  96.3 7.4 %collective-permute-start.3 = (bf16[20,6,1,320]{3,2,1,0:T(2,128)(2,1)S(1)}, bf16[20,6,1,320]{3,2,1,0:T(2,128)(2,1)S(1)}, u32[]{:S(2)}, u32[]{:S(2)}) collective-permute-start(bf16[20,6,1,320]{3,2,1,0:T(2,128)(2,1)S(1)} %get-tuple-element.20), channel_id=1, source_target_pairs={{2,0},{4,2},{6,4},{3,1},{5,3},{7,5},{10,8},{12,10},{14,12},{11,9},... | collective-permute-start | bytes 230408 | tf_op jit(solution)/shard_map/ppermute | solution.py:17
  97.6 7.6 %collective-permute-start.2 = (bf16[20,6,1,320]{3,2,1,0:T(2,128)(2,1)S(1)}, bf16[20,6,1,320]{3,2,1,0:T(2,128)(2,1)S(1)}, u32[]{:S(2)}, u32[]{:S(2)}) collective-permute-start(bf16[20,6,1,320]{3,2,1,0:T(2,128)(2,1)S(1)} %get-tuple-element.19), channel_id=1, source_target_pairs={{0,2},{2,4},{4,6},{1,3},{3,5},{5,7},{8,10},{10,12},{12,14},{9,11},... | collective-permute-start | bytes 230408 | tf_op jit(solution)/shard_map/ppermute | solution.py:14
  102.2 4.7 %copy-start.13 = (f32[4,320]{1,0:T(4,128)}, f32[4,320]{1,0:T(4,128)S(1)}, u32[]{:S(2)}) copy-start(f32[4,320]{1,0:T(4,128)S(1)} %get-tuple-element.35) | copy-start | bytes 15364
  103.7 3.2 %copy-start.7 = (bf16[20,6,1,320]{3,2,1,0:T(2,128)(2,1)}, bf16[20,6,1,320]{3,2,1,0:T(2,128)(2,1)S(1)}, u32[]{:S(2)}) copy-start(bf16[20,6,1,320]{3,2,1,0:T(2,128)(2,1)S(1)} %collective-permute-done.3) | copy-start | bytes 230404
  105.2 2.5 %copy-start.8 = (bf16[20,6,1,320]{3,2,1,0:T(2,128)(2,1)}, bf16[20,6,1,320]{3,2,1,0:T(2,128)(2,1)S(1)}, u32[]{:S(2)}) copy-start(bf16[20,6,1,320]{3,2,1,0:T(2,128)(2,1)S(1)} %collective-permute-done.2) | copy-start | bytes 230404
  121.6 6.3 %copy-start.12 = (bf16[64,320]{1,0:T(8,128)(2,1)S(1)}, bf16[64,320]{1,0:T(8,128)(2,1)}, u32[]{:S(2)}) copy-start(bf16[64,320]{1,0:T(8,128)(2,1)} %reshape.124) | copy-start | bytes 122884
  121.6 7.5 %copy-start.11 = (bf16[64,320]{1,0:T(8,128)(2,1)S(1)}, bf16[64,320]{1,0:T(8,128)(2,1)}, u32[]{:S(2)}) copy-start(bf16[64,320]{1,0:T(8,128)(2,1)} %reshape.125) | copy-start | bytes 122884
  121.6 8.7 %copy-start.9 = (bf16[64,320]{1,0:T(8,128)(2,1)S(1)}, bf16[64,320]{1,0:T(8,128)(2,1)}, u32[]{:S(2)}) copy-start(bf16[64,320]{1,0:T(8,128)(2,1)} %reshape.126) | copy-start | bytes 122884
  121.6 9.9 %copy-start.10 = (bf16[64,320]{1,0:T(8,128)(2,1)S(1)}, bf16[64,320]{1,0:T(8,128)(2,1)}, u32[]{:S(2)}) copy-start(bf16[64,320]{1,0:T(8,128)(2,1)} %reshape.127) | copy-start | bytes 122884
  155.3 3.1 %copy-start.1 = (bf16[9,320,640]{2,1,0:T(8,128)(2,1)S(1)}, bf16[9,320,640]{2,1,0:T(8,128)(2,1)}, u32[]{:S(2)}) copy-start(bf16[9,320,640]{2,1,0:T(8,128)(2,1)} %param.14) | copy-start | bytes 11059204
  155.3 4.5 %copy-start.6 = (bf16[256,320]{1,0:T(8,128)(2,1)S(1)}, bf16[256,320]{1,0:T(8,128)(2,1)}, u32[]{:S(2)}) copy-start(bf16[256,320]{1,0:T(8,128)(2,1)} %reshape.134) | copy-start | bytes 491524
  155.3 4.8 %copy-start.5 = (bf16[256,320]{1,0:T(8,128)(2,1)S(1)}, bf16[256,320]{1,0:T(8,128)(2,1)}, u32[]{:S(2)}) copy-start(bf16[256,320]{1,0:T(8,128)(2,1)} %reshape.135) | copy-start | bytes 491524
  156.9 3.6 %copy-start.4 = (bf16[256,320]{1,0:T(8,128)(2,1)S(1)}, bf16[256,320]{1,0:T(8,128)(2,1)}, u32[]{:S(2)}) copy-start(bf16[256,320]{1,0:T(8,128)(2,1)} %reshape.136) | copy-start | bytes 491524
  158.4 2.5 %copy-start.2 = (bf16[256,320]{1,0:T(8,128)(2,1)S(1)}, bf16[256,320]{1,0:T(8,128)(2,1)}, u32[]{:S(2)}) copy-start(bf16[256,320]{1,0:T(8,128)(2,1)} %reshape.137) | copy-start | bytes 491524
  159.7 1.5 copy-start.3
  160.5 46.1 %copy-start.14 = (f32[640]{0:T(1024)S(1)}, f32[640]{0:T(1024)}, u32[]{:S(2)}) copy-start(f32[640]{0:T(1024)} %param.15) | copy-start | bytes 7684
Sparse Core Ops, SparseCore 0:
  164.2 23.1 all-reduce.1

commit v2 on v0

--- a/solution.py
+++ b/solution.py
@@ -1,6 +1,10 @@
+import functools
+
 import jax
 import jax.numpy as jnp
 from jax import lax
+from jax.experimental import pallas as pl
+from jax.experimental.pallas import tpu as pltpu
 from jax.sharding import PartitionSpec as P
 
 GROUPS = 32
@@ -33,7 +37,7 @@
     return total
 
 
-def body(state, probe_signs, timesteps, time_table, gn_gain, gn_shift, conv_weight, conv_bias):
+def gathered_weights(state, probe_signs, timesteps, time_table, gn_gain, gn_shift, conv_weight, conv_bias):
     batch, tile_h, tile_w, chans = state.shape
     probes_here = probe_signs.shape[0]
     group_width = chans // GROUPS
@@ -86,7 +90,303 @@
     return (next_state, logp_delta)
 
 
+MESH = pl.DeviceIdType.MESH
+F32 = jnp.float32
+BF16 = jnp.bfloat16
+
+
+def exact_dot(a, b):
+    return jnp.dot(a, b, precision=lax.Precision.HIGHEST, preferred_element_type=F32)
+
+
+def kernel(
+    ny, nx, u_ref, x_ref, coef_ref, w_hbm, v_out, l_out,
+    w_ref, halo, same, other, peer, acts, line, plane, vel, vel_in, line2, plane2,
+    w_sem, send, recv,
+):
+    gy, gx, me = lax.axis_index("gy"), lax.axis_index("gx"), lax.axis_index("probe")
+    tile_h, tile_w, rows, chans = u_ref.shape
+    share = w_ref.shape[1]
+    batch = vel.shape[1]
+    cells = tile_h * tile_w
+    width = chans // GROUPS
+    count = cells * ny * nx * width
+    w_copy = pltpu.make_async_copy(w_hbm, w_ref, w_sem)
+    w_copy.start()
+
+    def half(array, which):
+        return jnp.where(which == 0, array, pltpu.roll(array, share, 1))[:, :share]
+
+    def spots(step, size, landing):
+        if step == 0:
+            return pl.ds(1, size) if landing else pl.ds(0, size)
+        if landing:
+            return pl.ds(0, 1) if step > 0 else pl.ds(size + 1, 1)
+        return pl.ds(size - 1, 1) if step > 0 else pl.ds(0, 1)
+
+    def exists(dy, dx):
+        y, x = gy + dy, gx + dx
+        return (y >= 0) & (y < ny) & (x >= 0) & (x < nx)
+
+    compass = [(dy, dx) for dy in (-1, 0, 1) for dx in (-1, 0, 1) if dy or dx]
+
+    for slot in range(3):
+        halo[slot] = jnp.zeros(halo.shape[1:], BF16)
+    barrier = pltpu.get_barrier_semaphore()
+    line_mates = [(gy, lax.rem(gx + k, nx), me) for k in range(1, nx)]
+    plane_mates = [
+        (lax.rem(gy + k, ny), gx, lax.rem(me + q, 2))
+        for k in range(ny) for q in range(2) if k or q
+    ]
+    extra = [(dy, dx, q) for dy, dx in compass for q in range(2) if dx and (dy or q)]
+    for mate in line_mates + plane_mates:
+        pl.semaphore_signal(barrier, inc=1, device_id=mate, device_id_type=MESH)
+    for dy, dx, q in extra:
+        @pl.when(exists(dy, dx))
+        def _():
+            pl.semaphore_signal(
+                barrier, inc=1, device_id=(gy + dy, gx + dx, lax.rem(me + q, 2)),
+                device_id_type=MESH,
+            )
+
+    u = u_ref[...].astype(F32).reshape(cells, rows, chans)
+    x = x_ref[...].astype(F32).reshape(cells, rows, chans)
+    box = (tile_h, tile_w, rows, share)
+    inner = (pl.ds(1, tile_h), pl.ds(1, tile_w))
+    x_mine = half(x.reshape(cells * rows, chans), me).reshape(box).astype(BF16)
+    u_flat = u.reshape(cells * rows, chans)
+    u_mine = half(u_flat, me).reshape(box).astype(BF16)
+    same[0] = x_mine
+    same[1] = u_mine
+    halo[(0,) + inner] = x_mine
+    halo[(1,) + inner] = u_mine
+    other[...] = half(u_flat, 1 - me).reshape(box).astype(BF16)
+    sums = jnp.concatenate(
+        [jnp.sum(x, 0), jnp.sum(x * x, 0), jnp.sum(u, 0), jnp.sum(u * x, 0)], axis=0
+    )
+    lanes = 128
+    chan = lax.broadcasted_iota(jnp.int32, (chans, lanes), 0)
+    group = lax.broadcasted_iota(jnp.int32, (chans, lanes), 1) * width
+    pick = ((chan >= group) & (chan < group + width)).astype(F32)
+    per_group = exact_dot(sums, pick)
+    local = per_group[:rows]
+    for k in range(1, 4):
+        local = local + pltpu.roll(per_group[k * rows : (k + 1) * rows], GROUPS * k, 1)
+    line[gx] = local
+
+    greeted = len(line_mates) + len(plane_mates)
+    for dy, dx, q in extra:
+        greeted = greeted + jnp.where(exists(dy, dx), 1, 0)
+    pl.semaphore_wait(barrier, greeted)
+
+    taken = [0]
+
+    def remote(src, dst, device):
+        taken[0] += 1
+        at = taken[0] - 1
+        return pltpu.make_async_remote_copy(
+            src_ref=src, dst_ref=dst, send_sem=send.at[at], recv_sem=recv.at[at],
+            device_id=device, device_id_type=MESH,
+        )
+
+    def to_all(src, dst, mates):
+        copies = [remote(src, dst, mate) for mate in mates]
+        for copy in copies:
+            copy.start()
+        return copies
+
+    line_copies = to_all(line.at[gx], line.at[gx], line_mates)
+    tile_copy = remote(u_ref, peer, (gy, gx, 1 - me))
+    tile_copy.start()
+    rims = []
+    for dy, dx in compass:
+        src = (spots(dy, tile_h, False), spots(dx, tile_w, False))
+        dst = (spots(dy, tile_h, True), spots(dx, tile_w, True))
+        both = [
+            remote(
+                same.at[(slice(None),) + src], halo.at[(pl.ds(0, 2),) + dst],
+                (gy + dy, gx + dx, me),
+            ),
+            remote(other.at[src], halo.at[(2,) + dst], (gy + dy, gx + dx, 1 - me)),
+        ]
+        rims.append((dy, dx, both))
+
+        @pl.when(exists(dy, dx))
+        def _():
+            for copy in both:
+                copy.start()
+
+    for copy in line_copies:
+        copy.wait()
+    total = line[0]
+    for k in range(1, nx):
+        total = total + line[k]
+    plane[gy, me] = total
+    plane_copies = to_all(plane.at[gy, me], plane.at[gy, me], plane_mates)
+    for copy in plane_copies:
+        copy.wait()
+
+    def moments(which):
+        total = plane[0, which]
+        for k in range(1, ny):
+            total = total + plane[k, which]
+        total = total / count
+        valid = lax.broadcasted_iota(jnp.int32, total.shape, 1) < GROUPS
+        return [
+            jnp.where(valid, total if k == 0 else pltpu.roll(total, lanes - GROUPS * k, 1), 0.0)
+            for k in range(4)
+        ]
+
+    mean_x, mean_xx, mean_u, cross = moments(me)
+    _, _, mean_v, cross_v = moments(1 - me)
+    inv = 1.0 / jnp.sqrt(mean_xx - mean_x * mean_x + 1e-05)
+    cube = inv * inv * inv
+    table = jnp.concatenate(
+        [mean_x, inv, mean_u, (cross - mean_x * mean_u) * cube, mean_v,
+         (cross_v - mean_x * mean_v) * cube], axis=0,
+    )
+    chan = lax.broadcasted_iota(jnp.int32, (lanes, share), 1) + me * share
+    group = lax.broadcasted_iota(jnp.int32, (lanes, share), 0) * width
+    spread = ((chan >= group) & (chan < group + width)).astype(F32)
+    table = exact_dot(table, spread)
+    mean_x, inv, mean_u, mean_cu, mean_v, mean_cv = [
+        table[k * rows : (k + 1) * rows] for k in range(6)
+    ]
+    coef = half(coef_ref[...], me)
+    offset, gain = coef[:rows], coef[rows:]
+
+    tile_copy.wait()
+    halo[(2,) + inner] = (
+        half(peer[...].astype(F32).reshape(cells * rows, chans), me).reshape(box).astype(BF16)
+    )
+    for dy, dx, both in rims:
+        @pl.when(exists(dy, dx))
+        def _():
+            for copy in both:
+                copy.wait_send()
+
+        @pl.when(exists(-dy, -dx))
+        def _():
+            for copy in both:
+                copy.wait_recv()
+
+    for y in range(tile_h + 2):
+        centered = halo[0, y].astype(F32) - mean_x
+        normal = centered * inv
+        pre = normal * gain + offset
+        sig = 1.0 / (1.0 + jnp.exp(-pre))
+        slope = sig * (1.0 + pre * (1.0 - sig)) * gain
+        acts[y, :, 0:rows] = pre * sig
+        acts[y, :, rows : 2 * rows] = slope * (
+            (halo[1, y].astype(F32) - mean_u) * inv - centered * mean_cu
+        )
+        acts[y, :, 2 * rows :] = slope * (
+            (halo[2, y].astype(F32) - mean_v) * inv - centered * mean_cv
+        )
+    for edge, at in (
+        (gy == 0, (0,)), (gy == ny - 1, (tile_h + 1,)),
+        (gx == 0, (slice(None), 0)), (gx == nx - 1, (slice(None), tile_w + 1)),
+    ):
+        @pl.when(edge)
+        def _():
+            acts[at] = jnp.zeros(acts.at[at].shape, F32)
+
+    def conv(first, size):
+        total = None
+        for tap in range(9):
+            dy, dx = tap // 3, tap % 3
+            window = acts[dy : dy + tile_h, dx : dx + tile_w, first : first + size]
+            window = window.reshape(cells * size, share).astype(BF16)
+            part = jnp.dot(window, w_ref[tap], preferred_element_type=F32)
+            total = part if total is None else total + part
+        return total.reshape(cells, size, chans)
+
+    w_copy.wait()
+    vel[...] = conv(0, rows)[:, :batch]
+    vel_copy = remote(vel, vel_in, (gy, gx, 1 - me))
+    vel_copy.start()
+    tangent = conv(rows, 2 * rows)
+    u = u_ref[...].astype(F32).reshape(cells, rows, chans)
+    v = peer[...].astype(F32).reshape(cells, rows, chans)
+    product = jnp.sum(u * tangent[:, :rows] + v * tangent[:, rows:], axis=0)
+    folded = product[:, :lanes]
+    for k in range(1, chans // lanes):
+        folded = folded + product[:, k * lanes : (k + 1) * lanes]
+    line2[gx] = folded
+    copies = to_all(line2.at[gx], line2.at[gx], line_mates)
+    for copy in copies:
+        copy.wait()
+    total = line2[0]
+    for k in range(1, nx):
+        total = total + line2[k]
+    plane2[gy, me] = total
+    copies = to_all(plane2.at[gy, me], plane2.at[gy, me], plane_mates)
+    vel_copy.wait()
+    v_out[...] = vel[...] + vel_in[...]
+    for copy in copies:
+        copy.wait()
+    total = None
+    for y in range(ny):
+        for q in range(2):
+            total = plane2[y, q] if total is None else total + plane2[y, q]
+    l_out[...] = total
+
+
+def one_kernel(state, probe_signs, timesteps, time_table, gn_gain, gn_shift, conv_weight, conv_bias):
+    batch, tile_h, tile_w, chans = state.shape
+    probes = probe_signs.shape[0]
+    share = conv_weight.shape[1]
+    ny, nx = lax.axis_size("gy"), lax.axis_size("gx")
+    rows = probes * batch
+    u = probe_signs.transpose(2, 3, 0, 1, 4).reshape(tile_h, tile_w, rows, chans).astype(BF16)
+    x = jnp.tile(state.transpose(1, 2, 0, 3), (1, 1, probes, 1))
+    embed = jnp.concatenate(
+        [lax.dynamic_slice_in_dim(time_table, timesteps[b], 1, 0) for b in range(batch)], axis=0
+    )
+    coef = jnp.concatenate(
+        [jnp.tile(embed + gn_shift, (probes, 1)), jnp.broadcast_to(gn_gain, (rows, chans))], axis=0
+    )
+    copies = 2 * (nx - 1) + 2 * (2 * ny - 1) + 2 + 16
+    vmem = pl.BlockSpec(memory_space=pltpu.VMEM)
+    velocity, partial = pl.pallas_call(
+        functools.partial(kernel, ny, nx),
+        out_shape=(
+            jax.ShapeDtypeStruct((tile_h * tile_w, batch, chans), F32),
+            jax.ShapeDtypeStruct((rows, 128), F32),
+        ),
+        in_specs=[vmem, vmem, vmem, pl.BlockSpec(memory_space=pl.ANY)],
+        out_specs=(vmem, vmem),
+        scratch_shapes=[
+            pltpu.VMEM(conv_weight.shape, BF16),
+            pltpu.VMEM((3, tile_h + 2, tile_w + 2, rows, share), BF16),
+            pltpu.VMEM((2, tile_h, tile_w, rows, share), BF16),
+            pltpu.VMEM((tile_h, tile_w, rows, share), BF16),
+            pltpu.VMEM((tile_h, tile_w, rows, chans), BF16),
+            pltpu.VMEM((tile_h + 2, tile_w + 2, 3 * rows, share), F32),
+            pltpu.VMEM((nx, rows, 128), F32),
+            pltpu.VMEM((ny, 2, rows, 128), F32),
+            pltpu.VMEM((tile_h * tile_w, batch, chans), F32),
+            pltpu.VMEM((tile_h * tile_w, batch, chans), F32),
+            pltpu.VMEM((nx, rows, 128), F32),
+            pltpu.VMEM((ny, 2, rows, 128), F32),
+            pltpu.SemaphoreType.DMA,
+            pltpu.SemaphoreType.DMA((copies,)),
+            pltpu.SemaphoreType.DMA((copies,)),
+        ],
+        compiler_params=pltpu.CompilerParams(collective_id=0, has_side_effects=True),
+    )(u, x, coef, conv_weight)
+    velocity = velocity.reshape(tile_h, tile_w, batch, chans).transpose(2, 0, 1, 3) + conv_bias
+    next_state = (state.astype(F32) + 0.25 * velocity).astype(BF16)
+    total = jnp.sum(partial.reshape(probes, batch, 128), axis=(0, 2))
+    return (next_state, -0.25 / (2 * probes) * total)
+
+
 def solution(mesh):
+    def body(*args):
+        wide = mesh.shape["probe"] == 2 and args[6].shape[1] >= 128
+        rows = args[1].shape[0] * args[0].shape[0]
+        return (one_kernel if wide and rows == 8 else gathered_weights)(*args)
+
     in_specs = (
         P(None, "gy", "gx", None),
         P("probe", None, "gy", "gx", None),

time: 172 us -> 46.3 us (0.27)
  blocking collectives: 103 us -> 0 us
  Pallas kernels: 0 us -> 26.8 us
  matrix products: 15.1 us -> 0 us
  local copies, waits for them, and re-layouts: 20 us -> 5.42 us
  starting transfers between devices: 7.62 us -> 0 us
  between operations: 14.5 us -> 8.33 us
  waiting for transfers between devices: 4.95 us -> 0 us
    psum x2 -> x0, blocking collectives: 103 us -> none  [the longest x1 63.3 us: body(): lax.psum((sum_x, sum_xx, sum_u, cross), ('gy', 'gx'))]
    pallas_call x0 -> x1, Pallas kernels: none -> 26.8 us  [one_kernel(): pl.pallas_call(functools.partial(kernel, ny, nx), out_shape=(jax.ShapeDty...]
    dot_general x10 -> x0, matrix products: 15.1 us -> none  [the longest x9 14.1 us: local_conv(): jnp.dot(window, weight[tap], preferred_element_type=jnp.float32)]
    reshape x10 -> x0, local copies, waits for them, and re-layouts: 13.9 us -> none  [the longest x9 13.8 us: local_conv(): padded[:, row_off:row_off + height, col_off:col_off + width, :]]
    ppermute x4 -> x0, starting transfers between devices: 7.58 us -> none  [the longest x2 5.01 us: with_halo(): lax.ppermute(lax.slice_in_dim(block, block.shape[dim] - width, None, axis...]
    ppermute x4 -> x0, waiting for transfers between devices: 4.27 us -> none  [the longest x2 3.4 us: with_halo(): lax.ppermute(lax.slice_in_dim(block, 0, width, axis=dim), axis, backward)]
    slice x5 -> x1, local copies, waits for them, and re-layouts: 4.23 us -> 1.47 us  [one_kernel(): timesteps[b]]
    concatenate x4 -> x1, other arithmetic: 3.23 us -> 0.62 us  [one_kernel(): jnp.concatenate([jnp.tile(embed + gn_shift, (probes, 1)), jnp.broadcast_t...]
  transfers between devices with their start and end apart: 5 -> 0, of which waited for: 2 -> 0; matrix products, arithmetic and copies ran while one was open for 14% -> 0% of each run, Pallas kernels for 0% -> 0%
where the time goes in v2:
time: 46.3 us; the launch traced here: 45.9 us
  Pallas kernels  26.8 us (58%)
  between operations  8.33 us (18%)
  local copies, waits for them, and re-layouts  5.42 us (12%)
  other arithmetic  5.31 us (11%)
    pallas_call x1, Pallas kernels, one_kernel(): pl.pallas_call(functools.partial(kernel, ny, nx), out_shape=(jax.ShapeDty...  26.8 us
    convert_element_type x1, other arithmetic, one_kernel(): next_state = (state.astype(F32) + 0.25 * velocity).astype(BF16)  1.61 us
    slice x1, local copies, waits for them, and re-layouts, one_kernel(): timesteps[b]  1.47 us
    convert_element_type x1, other arithmetic, one_kernel(): probe_signs.transpose(2, 3, 0, 1, 4).reshape(tile_h, tile_w, rows, chans)  1.03 us

profile of v2, /device:TPU:0, one launch (start us, length us, event | category | flops | bytes accessed | tf_op | source)
XLA Modules:
  0.0 45.9 jit_solution(12921488123572213043)
XLA Ops:
  0.6 1.5 %fusion.2 = (s32[1]{0:T(128)}, s32[1]{0:T(128)}, s32[1]{0:T(128)}, s32[1]{0:T(128)}) fusion(s32[4]{0:T(128)} %param.10), kind=kLoop, calls=%fused_computation.11 | loop fusion | bytes 32 | tf_op jit(solution)/shard_map/slice | solution.py:344
  9.7 0.8 %constant_dynamic-slice_fusion.3 = (f32[1,640]{1,0:T(1,128)S(1)}, f32[1,640]{1,0:T(1,128)S(1)}, f32[1,640]{1,0:T(1,128)S(1)}, f32[1,640]{1,0:T(1,128)S(1)}) fusion(f32[1000,640]{1,0:T(8,128)} %param.11, s32[]{:T(128)S(6)} %select_n.12, s32[]{:T(128)S(6)} %select_n.13, s32[]{:T(128)S(6)} %select_n.15, s32[]{:T(128)S(6)} %select_n.14), kind=kLoop, calls=%fused_computation.9 | loop fusion | bytes 20496 | tf_op jit(solution)/shard_map/dynamic_slice | solution.py:344
  10.5 0.7 %maximum_add_fusion = f32[4,640]{1,0:T(4,128)S(1)} fusion(f32[1,640]{1,0:T(1,128)S(1)} %get-tuple-element.8, f32[1,640]{1,0:T(1,128)S(1)} %get-tuple-element.9, f32[1,640]{1,0:T(1,128)S(1)} %get-tuple-element.7, f32[1,640]{1,0:T(1,128)S(1)} %get-tuple-element.6, f32[640]{0:T(1024)} %param.13), kind=kLoop, calls=%fused_computation.5 | loop fusion | flops 10240 | bytes 23040 | tf_op jit(solution)/shard_map/add | solution.py:347
  11.3 0.7 %broadcast_in_dim.2 = f32[8,640]{1,0:T(8,128)S(1)} broadcast(f32[640]{0:T(1024)} %param.12), dimensions={1} | broadcast | bytes 23040 | tf_op jit(solution)/shard_map/broadcast_in_dim | solution.py:347
  12.0 0.6 %pad_maximum_fusion.coef_ref = f32[16,640]{1,0:T(8,128)} fusion(f32[8,640]{1,0:T(8,128)S(1)} %broadcast_in_dim.2, f32[8,640]{1,0:T(8,128)S(1)} %tile.21), kind=kLoop, calls=%fused_computation.4 | loop fusion | flops 10240 | bytes 81920 | tf_op jit(solution)/shard_map/concatenate | solution.py:346
  12.6 0.9 %copy.11 = bf16[4,4,4,640]{3,2,1,0:T(4,128)(2,1)S(1)} copy(bf16[4,4,4,640]{3,1,0,2:T(4,128)(2,1)} %bitcast.14) | data formatting | bytes 163840 | tf_op jit(solution)/shard_map/transpose | solution.py:342
  13.6 0.0 copy-start
  13.6 0.0 copy-start.1
  13.6 0.7 %tile.9.x_ref = bf16[4,4,8,640]{3,2,1,0:T(8,128)(2,1)} reshape(bf16[4,4,2,4,640]{4,3,2,1,0:T(4,128)(2,1)S(1)} %tile.8) | data formatting | bytes 327680 | tf_op jit(solution)/shard_map/tile | solution.py:342
  14.3 1.0 %convert_element_type.14 = bf16[2,4,4,4,640]{4,3,2,1,0:T(4,128)(2,1)S(1)} convert(s32[2,4,4,4,640]{4,3,2,1,0:T(4,128)} %param.9) | non-fusion elementwise | flops 81920 | bytes 491520 | tf_op jit(solution)/shard_map/convert_element_type | solution.py:341
  15.3 0.7 %copy.13.u_ref = bf16[4,4,8,640]{3,2,1,0:T(8,128)(2,1)} copy(bf16[4,4,8,640]{3,1,0,2:T(4,128)(2,1)S(1)} %bitcast.13) | data formatting | bytes 327680 | tf_op jit(solution)/shard_map/convert_element_type | solution.py:341
  16.0 26.8 %shard_map.95 = (f32[16,4,640]{2,1,0:T(4,128)}, f32[8,128]{1,0:T(8,128)}) custom-call(bf16[4,4,8,640]{3,2,1,0:T(8,128)(2,1)} %copy.13.u_ref, bf16[4,4,8,640]{3,2,1,0:T(8,128)(2,1)} %tile.9.x_ref, f32[16,640]{1,0:T(8,128)} %pad_maximum_fusion.coef_ref, bf16[9,320,640]{2,1,0:T(8,128)(2,1)} %w_hbm.1), custom_call_target="tpu_custom_call" | custom-call | tf_op jit(solution)/shard_map/pallas_call | solution.py:351
  42.8 0.0 copy-done
  42.8 0.0 copy-done.1
  42.8 1.6 %fusion = bf16[4,4,4,640]{3,2,1,0:T(4,128)(2,1)} fusion(f32[4,4,4,640]{3,2,1,0:T(4,128)} %bitcast.15, bf16[4,4,4,640]{3,2,1,0:T(4,128)(2,1)S(1)} %copy-done, f32[640]{0:T(1024)S(1)} %copy-done.1), kind=kLoop, calls=%fused_computation.1 | loop fusion | flops 204800 | bytes 330240 | tf_op jit(solution)/shard_map/convert_element_type | solution.py:379
  44.4 0.8 %reduce_sum.10 = f32[8]{0:T(128)S(1)} reduce(f32[8,128]{1,0:T(8,128)} %get-tuple-element.5, f32[]{:T(128)} %constant.3.clone.1), dimensions={1}, to_apply=%region_0.0 | reduce | flops 1016 | bytes 4132 | tf_op jit(solution)/shard_map/reduce_sum | solution.py:380
  45.2 0.1 reduce_sum.14
  45.3 0.5 %broadcast_multiply_fusion = f32[4]{0:T(128)} fusion(f32[4]{0:T(128)S(1)} %reduce_sum.18), kind=kLoop, calls=%fused_computation.10 | loop fusion | flops 4 | bytes 32 | tf_op jit(solution)/shard_map/mul | solution.py:381
  (4 shorter events, 0.1 us)
Async XLA Ops:
  13.6 29.2 %copy-start = (bf16[4,4,4,640]{3,2,1,0:T(4,128)(2,1)S(1)}, bf16[4,4,4,640]{3,2,1,0:T(4,128)(2,1)}, u32[]{:S(2)}) copy-start(bf16[4,4,4,640]{3,2,1,0:T(4,128)(2,1)} %param.8) | copy-start | bytes 245764
  13.6 29.2 %copy-start.1 = (f32[640]{0:T(1024)S(1)}, f32[640]{0:T(1024)}, u32[]{:S(2)}) copy-start(f32[640]{0:T(1024)} %param.15) | copy-start | bytes 7684

commit v3 on v2

--- a/solution.py
+++ b/solution.py
@@ -100,18 +100,21 @@
 
 
 def kernel(
-    ny, nx, u_ref, x_ref, coef_ref, w_hbm, v_out, l_out,
-    w_ref, halo, same, other, peer, acts, line, plane, vel, vel_in, line2, plane2,
-    w_sem, send, recv,
+    ny, nx, steps_ref, state_ref, signs_ref, time_hbm, gain_ref, shift_ref, bias_ref, w_hbm,
+    out, l_out,
+    time_ref, w_ref, state_f, halo, same, other, rest, acts, line, plane, vel, vel_in, parts,
+    t_sem, w_sem, send, recv,
 ):
     gy, gx, me = lax.axis_index("gy"), lax.axis_index("gx"), lax.axis_index("probe")
-    tile_h, tile_w, rows, chans = u_ref.shape
+    probes, batch, tile_h, tile_w, chans = signs_ref.shape
+    rows = probes * batch
     share = w_ref.shape[1]
-    batch = vel.shape[1]
     cells = tile_h * tile_w
     width = chans // GROUPS
     count = cells * ny * nx * width
     w_copy = pltpu.make_async_copy(w_hbm, w_ref, w_sem)
+    time_copy = pltpu.make_async_copy(time_hbm, time_ref, t_sem)
+    time_copy.start()
     w_copy.start()
 
     def half(array, which):
@@ -149,8 +152,14 @@
                 device_id_type=MESH,
             )
 
-    u = u_ref[...].astype(F32).reshape(cells, rows, chans)
-    x = x_ref[...].astype(F32).reshape(cells, rows, chans)
+    state_f[...] = state_ref[...].astype(F32)
+    spot_list = [(y, w) for y in range(tile_h) for w in range(tile_w)]
+    u = jnp.stack(
+        [signs_ref[:, :, y, w, :].reshape(rows, chans) for y, w in spot_list]
+    ).astype(F32)
+    x = jnp.stack(
+        [jnp.concatenate([state_f[:, y, w, :]] * probes, axis=0) for y, w in spot_list]
+    )
     box = (tile_h, tile_w, rows, share)
     inner = (pl.ds(1, tile_h), pl.ds(1, tile_w))
     x_mine = half(x.reshape(cells * rows, chans), me).reshape(box).astype(BF16)
@@ -196,7 +205,7 @@
         return copies
 
     line_copies = to_all(line.at[gx], line.at[gx], line_mates)
-    tile_copy = remote(u_ref, peer, (gy, gx, 1 - me))
+    tile_copy = remote(other, halo.at[(2,) + inner], (gy, gx, 1 - me))
     tile_copy.start()
     rims = []
     for dy, dx in compass:
@@ -216,6 +225,9 @@
             for copy in both:
                 copy.start()
 
+    rest_copy = remote(same.at[1], rest, (gy, gx, 1 - me))
+    rest_copy.start()
+
     for copy in line_copies:
         copy.wait()
     total = line[0]
@@ -252,13 +264,14 @@
     mean_x, inv, mean_u, mean_cu, mean_v, mean_cv = [
         table[k * rows : (k + 1) * rows] for k in range(6)
     ]
-    coef = half(coef_ref[...], me)
-    offset, gain = coef[:rows], coef[rows:]
+    time_copy.wait()
+    embed = jnp.concatenate(
+        [time_ref[pl.ds(steps_ref[b], 1), :] for b in range(batch)] * probes, axis=0
+    )
+    offset = half(embed + shift_ref[...].reshape(1, chans), me)
+    gain = half(jnp.broadcast_to(gain_ref[...].reshape(1, chans), (rows, chans)), me)
 
     tile_copy.wait()
-    halo[(2,) + inner] = (
-        half(peer[...].astype(F32).reshape(cells * rows, chans), me).reshape(box).astype(BF16)
-    )
     for dy, dx, both in rims:
         @pl.when(exists(dy, dx))
         def _():
@@ -305,31 +318,39 @@
     vel[...] = conv(0, rows)[:, :batch]
     vel_copy = remote(vel, vel_in, (gy, gx, 1 - me))
     vel_copy.start()
-    tangent = conv(rows, 2 * rows)
-    u = u_ref[...].astype(F32).reshape(cells, rows, chans)
-    v = peer[...].astype(F32).reshape(cells, rows, chans)
-    product = jnp.sum(u * tangent[:, :rows] + v * tangent[:, rows:], axis=0)
-    folded = product[:, :lanes]
-    for k in range(1, chans // lanes):
-        folded = folded + product[:, k * lanes : (k + 1) * lanes]
-    line2[gx] = folded
-    copies = to_all(line2.at[gx], line2.at[gx], line_mates)
+    tangent = conv(rows, 2 * rows).reshape(cells * 2 * rows, chans)
+    rest_copy.wait()
+
+    def pairs(at):
+        return at.astype(F32).reshape(cells, rows, share)
+
+    near = half(tangent, me).reshape(cells, 2 * rows, share)
+    far = half(tangent, 1 - me).reshape(cells, 2 * rows, share)
+    product = jnp.sum(
+        pairs(same[1]) * near[:, :rows] + pairs(halo[(2,) + inner]) * near[:, rows:]
+        + pairs(other[...]) * far[:, :rows] + pairs(rest[...]) * far[:, rows:],
+        axis=0,
+    )
+    product = jnp.sum(product, axis=1, keepdims=True)
+    lane = lax.broadcasted_iota(jnp.int32, (rows, lanes), 1)
+    row = lax.broadcasted_iota(jnp.int32, (rows, lanes), 0)
+    here = jnp.where(lane == lax.rem(row, batch), product, 0.0)
+    mine = (gy * nx + gx) * 2 + me
+    parts[mine] = jnp.sum(here, axis=0, keepdims=True)
+    everyone = [
+        (lax.rem(gy + a, ny), lax.rem(gx + b, nx), lax.rem(me + q, 2))
+        for a in range(ny) for b in range(nx) for q in range(2) if a or b or q
+    ]
+    copies = to_all(parts.at[mine], parts.at[mine], everyone)
+    vel_copy.wait()
+    vel[...] = 0.25 * (vel[...] + vel_in[...] + bias_ref[...].reshape(1, chans))
+    for b in range(batch):
+        for y in range(tile_h):
+            moved = vel[y * tile_w : (y + 1) * tile_w, b, :]
+            out[b, y] = (state_f[b, y] + moved).astype(BF16)
     for copy in copies:
         copy.wait()
-    total = line2[0]
-    for k in range(1, nx):
-        total = total + line2[k]
-    plane2[gy, me] = total
-    copies = to_all(plane2.at[gy, me], plane2.at[gy, me], plane_mates)
-    vel_copy.wait()
-    v_out[...] = vel[...] + vel_in[...]
-    for copy in copies:
-        copy.wait()
-    total = None
-    for y in range(ny):
-        for q in range(2):
-            total = plane2[y, q] if total is None else total + plane2[y, q]
-    l_out[...] = total
+    l_out[...] = jnp.sum(parts[...], axis=0) * (-0.25 / (2 * probes))
 
 
 def one_kernel(state, probe_signs, timesteps, time_table, gn_gain, gn_shift, conv_weight, conv_bias):
@@ -338,47 +359,45 @@
     share = conv_weight.shape[1]
     ny, nx = lax.axis_size("gy"), lax.axis_size("gx")
     rows = probes * batch
-    u = probe_signs.transpose(2, 3, 0, 1, 4).reshape(tile_h, tile_w, rows, chans).astype(BF16)
-    x = jnp.tile(state.transpose(1, 2, 0, 3), (1, 1, probes, 1))
-    embed = jnp.concatenate(
-        [lax.dynamic_slice_in_dim(time_table, timesteps[b], 1, 0) for b in range(batch)], axis=0
-    )
-    coef = jnp.concatenate(
-        [jnp.tile(embed + gn_shift, (probes, 1)), jnp.broadcast_to(gn_gain, (rows, chans))], axis=0
-    )
-    copies = 2 * (nx - 1) + 2 * (2 * ny - 1) + 2 + 16
+    cells = tile_h * tile_w
+    copies = (nx - 1) + (2 * ny - 1) + 3 + 16 + (2 * nx * ny - 1)
     vmem = pl.BlockSpec(memory_space=pltpu.VMEM)
-    velocity, partial = pl.pallas_call(
+    hbm = pl.BlockSpec(memory_space=pl.ANY)
+    next_state, total = pl.pallas_call(
         functools.partial(kernel, ny, nx),
         out_shape=(
-            jax.ShapeDtypeStruct((tile_h * tile_w, batch, chans), F32),
-            jax.ShapeDtypeStruct((rows, 128), F32),
+            jax.ShapeDtypeStruct(state.shape, BF16),
+            jax.ShapeDtypeStruct((1, 128), F32),
         ),
-        in_specs=[vmem, vmem, vmem, pl.BlockSpec(memory_space=pl.ANY)],
+        in_specs=[
+            pl.BlockSpec(memory_space=pltpu.SMEM), vmem, vmem, hbm, vmem, vmem, vmem, hbm
+        ],
         out_specs=(vmem, vmem),
         scratch_shapes=[
+            pltpu.VMEM(time_table.shape, F32),
             pltpu.VMEM(conv_weight.shape, BF16),
+            pltpu.VMEM(state.shape, F32),
             pltpu.VMEM((3, tile_h + 2, tile_w + 2, rows, share), BF16),
             pltpu.VMEM((2, tile_h, tile_w, rows, share), BF16),
             pltpu.VMEM((tile_h, tile_w, rows, share), BF16),
-            pltpu.VMEM((tile_h, tile_w, rows, chans), BF16),
+            pltpu.VMEM((tile_h, tile_w, rows, share), BF16),
             pltpu.VMEM((tile_h + 2, tile_w + 2, 3 * rows, share), F32),
             pltpu.VMEM((nx, rows, 128), F32),
             pltpu.VMEM((ny, 2, rows, 128), F32),
-            pltpu.VMEM((tile_h * tile_w, batch, chans), F32),
-            pltpu.VMEM((tile_h * tile_w, batch, chans), F32),
-            pltpu.VMEM((nx, rows, 128), F32),
-            pltpu.VMEM((ny, 2, rows, 128), F32),
+            pltpu.VMEM((cells, batch, chans), F32),
+            pltpu.VMEM((cells, batch, chans), F32),
+            pltpu.VMEM((2 * nx * ny, 1, 128), F32),
+            pltpu.SemaphoreType.DMA,
             pltpu.SemaphoreType.DMA,
             pltpu.SemaphoreType.DMA((copies,)),
             pltpu.SemaphoreType.DMA((copies,)),
         ],
         compiler_params=pltpu.CompilerParams(collective_id=0, has_side_effects=True),
-    )(u, x, coef, conv_weight)
-    velocity = velocity.reshape(tile_h, tile_w, batch, chans).transpose(2, 0, 1, 3) + conv_bias
-    next_state = (state.astype(F32) + 0.25 * velocity).astype(BF16)
-    total = jnp.sum(partial.reshape(probes, batch, 128), axis=(0, 2))
-    return (next_state, -0.25 / (2 * probes) * total)
+    )(
+        timesteps, state, probe_signs, time_table, gn_gain,
+        gn_shift, conv_bias, conv_weight,
+    )
+    return (next_state, total[0, :batch])
 
 
 def solution(mesh):

time: 46.3 us -> 29.5 us (0.64)
  between operations: 8.33 us -> 0.64 us
  other arithmetic: 5.31 us -> 0 us
  local copies, waits for them, and re-layouts: 5.42 us -> 2.66 us
  Pallas kernels: 26.8 us -> 26 us
    convert_element_type x2 -> x0, other arithmetic: 2.64 us -> none  [the longest x1 1.61 us: one_kernel(): next_state = (state.astype(F32) + 0.25 * velocity).astype(BF16)]
    unnamed x4 -> x1, local copies, waits for them, and re-layouts: 0.01 us -> 1.55 us
    slice x1 -> x0, local copies, waits for them, and re-layouts: 1.47 us -> none  [one_kernel(): timesteps[b]]
    squeeze x0 -> x1, local copies, waits for them, and re-layouts: none -> 1.11 us  [one_kernel(): return (next_state, total[0, :batch])]
    transpose x1 -> x0, local copies, waits for them, and re-layouts: 0.92 us -> none  [one_kernel(): x = jnp.tile(state.transpose(1, 2, 0, 3), (1, 1, probes, 1))]
    reduce_sum x2 -> x0, other arithmetic: 0.82 us -> none  [one_kernel(): total = jnp.sum(partial.reshape(probes, batch, 128), axis=(0, 2))]
    dynamic_slice x1 -> x0, local copies, waits for them, and re-layouts: 0.8 us -> none  [one_kernel(): lax.dynamic_slice_in_dim(time_table, timesteps[b], 1, 0)]
    pallas_call x1, Pallas kernels: 26.8 us -> 26 us  [one_kernel(): pl.pallas_call(functools.partial(kernel, ny, nx), out_shape=(jax.ShapeDty...]
where the time goes in v3:
time: 29.5 us; the launch traced here: 29.3 us
  Pallas kernels  26 us (88%)
  local copies, waits for them, and re-layouts  2.66 us (9%)
  between operations  0.64 us (2%)
    pallas_call x1, Pallas kernels, one_kernel(): pl.pallas_call(functools.partial(kernel, ny, nx), out_shape=(jax.ShapeDty...  26 us
    unnamed x1, local copies, waits for them, and re-layouts  1.55 us
    squeeze x1, local copies, waits for them, and re-layouts, one_kernel(): return (next_state, total[0, :batch])  1.11 us

profile of v3, /device:TPU:0, one launch (start us, length us, event | category | flops | bytes accessed | tf_op | source)
XLA Modules:
  0.0 29.3 jit_solution(15344811930327058882)
XLA Ops:
  0.6 26.0 %shard_map.95 = (bf16[4,4,4,640]{3,2,1,0:T(4,128)(2,1)}, f32[1,128]{1,0:T(1,128)}) custom-call(s32[4]{0:T(128)} %steps_ref.1, bf16[4,4,4,640]{3,2,1,0:T(4,128)(2,1)} %state_ref.1, s32[2,4,4,4,640]{4,3,2,1,0:T(4,128)} %signs_ref.1, f32[1000,640]{1,0:T(8,128)} %time_hbm.1, f32[640]{0:T(1024)} %gain_ref.1, f32[640]{0:T(1024)} %shift_ref.1, f32[640]{0:T(1024)} %bias_ref.1, ...), custom_call_target="tpu_custom_call" | custom-call | tf_op jit(solution)/shard_map/pallas_call | solution.py:366
  26.6 1.1 %slice_bitcast_fusion = f32[4]{0:T(128)} fusion(f32[1,128]{1,0:T(1,128)} %get-tuple-element.5), kind=kLoop, calls=%fused_computation | loop fusion | bytes 32 | tf_op jit(solution)/shard_map/squeeze | solution.py:400
  27.7 1.6 %copy.11 = bf16[4,4,4,640]{3,2,1,0:T(4,128)(2,1)} copy(bf16[4,4,4,640]{3,2,1,0:T(4,128)(2,1)} %get-tuple-element.8) | data formatting | bytes 163840

commit v4 on v3

--- a/solution.py
+++ b/solution.py
@@ -100,10 +100,10 @@
 
 
 def kernel(
-    ny, nx, steps_ref, state_ref, signs_ref, time_hbm, gain_ref, shift_ref, bias_ref, w_hbm,
+    ny, nx, steps_ref, state_hbm, signs_hbm, time_hbm, gain_hbm, shift_hbm, bias_hbm, w_hbm,
     out, l_out,
-    time_ref, w_ref, state_f, halo, same, other, rest, acts, line, plane, vel, vel_in, parts,
-    t_sem, w_sem, send, recv,
+    state_ref, signs_ref, time_ref, gain_ref, shift_ref, bias_ref, w_ref, state_f, halo, same, other, rest, acts, line, plane, vel, vel_in, parts,
+    fetched, send, recv,
 ):
     gy, gx, me = lax.axis_index("gy"), lax.axis_index("gx"), lax.axis_index("probe")
     probes, batch, tile_h, tile_w, chans = signs_ref.shape
@@ -112,10 +112,13 @@
     cells = tile_h * tile_w
     width = chans // GROUPS
     count = cells * ny * nx * width
-    w_copy = pltpu.make_async_copy(w_hbm, w_ref, w_sem)
-    time_copy = pltpu.make_async_copy(time_hbm, time_ref, t_sem)
-    time_copy.start()
-    w_copy.start()
+    inputs = [
+        pltpu.make_async_copy(src, dst, fetched.at[at])
+        for at, (src, dst) in enumerate([
+            (state_hbm, state_ref), (signs_hbm, signs_ref), (time_hbm, time_ref),
+            (gain_hbm, gain_ref), (shift_hbm, shift_ref), (bias_hbm, bias_ref), (w_hbm, w_ref),
+        ])
+    ]
 
     def half(array, which):
         return jnp.where(which == 0, array, pltpu.roll(array, share, 1))[:, :share]
@@ -133,8 +136,6 @@
 
     compass = [(dy, dx) for dy in (-1, 0, 1) for dx in (-1, 0, 1) if dy or dx]
 
-    for slot in range(3):
-        halo[slot] = jnp.zeros(halo.shape[1:], BF16)
     barrier = pltpu.get_barrier_semaphore()
     line_mates = [(gy, lax.rem(gx + k, nx), me) for k in range(1, nx)]
     plane_mates = [
@@ -152,6 +153,11 @@
                 device_id_type=MESH,
             )
 
+    for copy in inputs:
+        copy.start()
+
+    inputs[0].wait()
+    inputs[1].wait()
     state_f[...] = state_ref[...].astype(F32)
     spot_list = [(y, w) for y in range(tile_h) for w in range(tile_w)]
     u = jnp.stack(
@@ -181,7 +187,7 @@
     local = per_group[:rows]
     for k in range(1, 4):
         local = local + pltpu.roll(per_group[k * rows : (k + 1) * rows], GROUPS * k, 1)
-    line[gx] = local
+    plane[gy, me] = local
 
     greeted = len(line_mates) + len(plane_mates)
     for dy, dx, q in extra:
@@ -204,7 +210,7 @@
             copy.start()
         return copies
 
-    line_copies = to_all(line.at[gx], line.at[gx], line_mates)
+    plane_copies = to_all(plane.at[gy, me], plane.at[gy, me], plane_mates)
     tile_copy = remote(other, halo.at[(2,) + inner], (gy, gx, 1 - me))
     tile_copy.start()
     rims = []
@@ -225,23 +231,23 @@
             for copy in both:
                 copy.start()
 
-    rest_copy = remote(same.at[1], rest, (gy, gx, 1 - me))
-    rest_copy.start()
-
-    for copy in line_copies:
-        copy.wait()
-    total = line[0]
-    for k in range(1, nx):
-        total = total + line[k]
-    plane[gy, me] = total
-    plane_copies = to_all(plane.at[gy, me], plane.at[gy, me], plane_mates)
     for copy in plane_copies:
         copy.wait()
-
-    def moments(which):
+    for which in range(2):
         total = plane[0, which]
         for k in range(1, ny):
             total = total + plane[k, which]
+        line[gx, which] = total
+    line_copies = to_all(line.at[gx], line.at[gx], line_mates)
+    rest_copy = remote(same.at[1], rest, (gy, gx, 1 - me))
+    rest_copy.start()
+    for copy in line_copies:
+        copy.wait()
+
+    def moments(which):
+        total = line[0, which]
+        for k in range(1, nx):
+            total = total + line[k, which]
         total = total / count
         valid = lax.broadcasted_iota(jnp.int32, total.shape, 1) < GROUPS
         return [
@@ -264,7 +270,8 @@
     mean_x, inv, mean_u, mean_cu, mean_v, mean_cv = [
         table[k * rows : (k + 1) * rows] for k in range(6)
     ]
-    time_copy.wait()
+    for copy in inputs[2:6]:
+        copy.wait()
     embed = jnp.concatenate(
         [time_ref[pl.ds(steps_ref[b], 1), :] for b in range(batch)] * probes, axis=0
     )
@@ -314,7 +321,7 @@
             total = part if total is None else total + part
         return total.reshape(cells, size, chans)
 
-    w_copy.wait()
+    inputs[6].wait()
     vel[...] = conv(0, rows)[:, :batch]
     vel_copy = remote(vel, vel_in, (gy, gx, 1 - me))
     vel_copy.start()
@@ -369,12 +376,15 @@
             jax.ShapeDtypeStruct(state.shape, BF16),
             jax.ShapeDtypeStruct((1, 128), F32),
         ),
-        in_specs=[
-            pl.BlockSpec(memory_space=pltpu.SMEM), vmem, vmem, hbm, vmem, vmem, vmem, hbm
-        ],
+        in_specs=[pl.BlockSpec(memory_space=pltpu.SMEM)] + [hbm] * 7,
         out_specs=(vmem, vmem),
         scratch_shapes=[
+            pltpu.VMEM(state.shape, BF16),
+            pltpu.VMEM(probe_signs.shape, jnp.int32),
             pltpu.VMEM(time_table.shape, F32),
+            pltpu.VMEM(gn_gain.shape, F32),
+            pltpu.VMEM(gn_shift.shape, F32),
+            pltpu.VMEM(conv_bias.shape, F32),
             pltpu.VMEM(conv_weight.shape, BF16),
             pltpu.VMEM(state.shape, F32),
             pltpu.VMEM((3, tile_h + 2, tile_w + 2, rows, share), BF16),
@@ -382,13 +392,12 @@
             pltpu.VMEM((tile_h, tile_w, rows, share), BF16),
             pltpu.VMEM((tile_h, tile_w, rows, share), BF16),
             pltpu.VMEM((tile_h + 2, tile_w + 2, 3 * rows, share), F32),
-            pltpu.VMEM((nx, rows, 128), F32),
+            pltpu.VMEM((nx, 2, rows, 128), F32),
             pltpu.VMEM((ny, 2, rows, 128), F32),
             pltpu.VMEM((cells, batch, chans), F32),
             pltpu.VMEM((cells, batch, chans), F32),
             pltpu.VMEM((2 * nx * ny, 1, 128), F32),
-            pltpu.SemaphoreType.DMA,
-            pltpu.SemaphoreType.DMA,
+            pltpu.SemaphoreType.DMA((7,)),
             pltpu.SemaphoreType.DMA((copies,)),
             pltpu.SemaphoreType.DMA((copies,)),
         ],

time: 29.5 us -> 27.2 us (0.922)
  Pallas kernels: 26 us -> 23.8 us
    pallas_call x1, Pallas kernels: 26 us -> 23.8 us  [one_kernel(): pl.pallas_call(functools.partial(kernel, ny, nx), out_shape=(jax.ShapeDty...]
where the time goes in v4:
time: 27.2 us; the launch traced here: 27.1 us
  Pallas kernels  23.8 us (88%)
  local copies, waits for them, and re-layouts  2.66 us (10%)
  between operations  0.64 us (2%)
    pallas_call x1, Pallas kernels, one_kernel(): pl.pallas_call(functools.partial(kernel, ny, nx), out_shape=(jax.ShapeDty...  23.8 us
    unnamed x1, local copies, waits for them, and re-layouts  1.55 us
    squeeze x1, local copies, waits for them, and re-layouts, one_kernel(): return (next_state, total[0, :batch])  1.11 us

profile of v4, /device:TPU:0, one launch (start us, length us, event | category | flops | bytes accessed | tf_op | source)
XLA Modules:
  0.0 27.1 jit_solution(14879099650142257856)
XLA Ops:
  0.6 23.8 %shard_map.95 = (bf16[4,4,4,640]{3,2,1,0:T(4,128)(2,1)}, f32[1,128]{1,0:T(1,128)}) custom-call(s32[4]{0:T(128)} %steps_ref.1, bf16[4,4,4,640]{3,2,1,0:T(4,128)(2,1)} %state_hbm.1, s32[2,4,4,4,640]{4,3,2,1,0:T(4,128)} %signs_hbm.1, f32[1000,640]{1,0:T(8,128)} %time_hbm.1, f32[640]{0:T(1024)} %gain_hbm.1, f32[640]{0:T(1024)} %shift_hbm.1, f32[640]{0:T(1024)} %bias_hbm.1, ...), custom_call_target="tpu_custom_call" | custom-call | tf_op jit(solution)/shard_map/pallas_call | solution.py:373
  24.4 1.1 %slice_bitcast_fusion = f32[4]{0:T(128)} fusion(f32[1,128]{1,0:T(1,128)} %get-tuple-element.5), kind=kLoop, calls=%fused_computation | loop fusion | bytes 32 | tf_op jit(solution)/shard_map/squeeze | solution.py:409
  25.5 1.6 %copy.11 = bf16[4,4,4,640]{3,2,1,0:T(4,128)(2,1)} copy(bf16[4,4,4,640]{3,2,1,0:T(4,128)(2,1)} %get-tuple-element.8) | data formatting | bytes 163840

commit v5 on v4

--- a/solution.py
+++ b/solution.py
@@ -102,13 +102,13 @@
 def kernel(
     ny, nx, steps_ref, state_hbm, signs_hbm, time_hbm, gain_hbm, shift_hbm, bias_hbm, w_hbm,
     out, l_out,
-    state_ref, signs_ref, time_ref, gain_ref, shift_ref, bias_ref, w_ref, state_f, halo, same, other, rest, acts, line, plane, vel, vel_in, parts,
+    state_ref, signs_ref, time_ref, gain_ref, shift_ref, bias_ref, w_ref, state_f, halo, same, other, rest, acts, cols, line, plane, vel, vel_in, parts,
     fetched, send, recv,
 ):
     gy, gx, me = lax.axis_index("gy"), lax.axis_index("gx"), lax.axis_index("probe")
     probes, batch, tile_h, tile_w, chans = signs_ref.shape
     rows = probes * batch
-    share = w_ref.shape[1]
+    share = w_ref.shape[0] // 9
     cells = tile_h * tile_w
     width = chans // GROUPS
     count = cells * ny * nx * width
@@ -312,13 +312,13 @@
             acts[at] = jnp.zeros(acts.at[at].shape, F32)
 
     def conv(first, size):
-        total = None
         for tap in range(9):
             dy, dx = tap // 3, tap % 3
             window = acts[dy : dy + tile_h, dx : dx + tile_w, first : first + size]
-            window = window.reshape(cells * size, share).astype(BF16)
-            part = jnp.dot(window, w_ref[tap], preferred_element_type=F32)
-            total = part if total is None else total + part
+            cols[: cells * size, tap * share : (tap + 1) * share] = window.reshape(
+                cells * size, share
+            ).astype(BF16)
+        total = jnp.dot(cols[: cells * size], w_ref[...], preferred_element_type=F32)
         return total.reshape(cells, size, chans)
 
     inputs[6].wait()
@@ -358,6 +358,11 @@
     for copy in copies:
         copy.wait()
     l_out[...] = jnp.sum(parts[...], axis=0) * (-0.25 / (2 * probes))
+
+
+def settle(state_ref, total_ref, state_out, total_out):
+    state_out[...] = state_ref[...]
+    total_out[...] = total_ref[0, : total_out.shape[0]]
 
 
 def one_kernel(state, probe_signs, timesteps, time_table, gn_gain, gn_shift, conv_weight, conv_bias):
@@ -385,13 +390,14 @@
             pltpu.VMEM(gn_gain.shape, F32),
             pltpu.VMEM(gn_shift.shape, F32),
             pltpu.VMEM(conv_bias.shape, F32),
-            pltpu.VMEM(conv_weight.shape, BF16),
+            pltpu.VMEM((9 * share, chans), BF16),
             pltpu.VMEM(state.shape, F32),
             pltpu.VMEM((3, tile_h + 2, tile_w + 2, rows, share), BF16),
             pltpu.VMEM((2, tile_h, tile_w, rows, share), BF16),
             pltpu.VMEM((tile_h, tile_w, rows, share), BF16),
             pltpu.VMEM((tile_h, tile_w, rows, share), BF16),
             pltpu.VMEM((tile_h + 2, tile_w + 2, 3 * rows, share), F32),
+            pltpu.VMEM((cells * 2 * rows, 9 * share), BF16),
             pltpu.VMEM((nx, 2, rows, 128), F32),
             pltpu.VMEM((ny, 2, rows, 128), F32),
             pltpu.VMEM((cells, batch, chans), F32),
@@ -404,9 +410,17 @@
         compiler_params=pltpu.CompilerParams(collective_id=0, has_side_effects=True),
     )(
         timesteps, state, probe_signs, time_table, gn_gain,
-        gn_shift, conv_bias, conv_weight,
-    )
-    return (next_state, total[0, :batch])
+        gn_shift, conv_bias,
+        conv_weight.reshape(9 * share, chans),
+    )
+    return pl.pallas_call(
+        settle,
+        out_shape=(
+            jax.ShapeDtypeStruct(state.shape, BF16), jax.ShapeDtypeStruct((batch,), F32)
+        ),
+        in_specs=[vmem, vmem],
+        out_specs=(vmem, vmem),
+    )(next_state, total)
 
 
 def solution(mesh):

time: 27.2 us -> 24.8 us (0.912)
  local copies, waits for them, and re-layouts: 2.66 us -> 0 us
    unnamed x1 -> x0, local copies, waits for them, and re-layouts: 1.55 us -> none
    pallas_call x0 -> x1, Pallas kernels: none -> 1.54 us  [one_kernel(): pl.pallas_call(settle, out_shape=(jax.ShapeDtypeStruct(state.shape, BF16)...]
    pallas_call x1, Pallas kernels: 23.8 us -> 22.5 us  [one_kernel(): pl.pallas_call(functools.partial(kernel, ny, nx), out_shape=(jax.ShapeDty...]
    squeeze x1 -> x0, local copies, waits for them, and re-layouts: 1.11 us -> none  [one_kernel(): return (next_state, total[0, :batch])]
where the time goes in v5:
time: 24.8 us; the launch traced here: 24.7 us
  Pallas kernels  24 us (97%)
  between operations  0.64 us (3%)
    pallas_call x1, Pallas kernels, one_kernel(): pl.pallas_call(functools.partial(kernel, ny, nx), out_shape=(jax.ShapeDty...  22.5 us
    pallas_call x1, Pallas kernels, one_kernel(): pl.pallas_call(settle, out_shape=(jax.ShapeDtypeStruct(state.shape, BF16)...  1.54 us

profile of v5, /device:TPU:0, one launch (start us, length us, event | category | flops | bytes accessed | tf_op | source)
XLA Modules:
  0.0 24.7 jit_solution(13769900822375880666)
XLA Ops:
  0.6 22.5 %shard_map.95 = (bf16[4,4,4,640]{3,2,1,0:T(4,128)(2,1)}, f32[1,128]{1,0:T(1,128)}) custom-call(s32[4]{0:T(128)} %steps_ref.1, bf16[4,4,4,640]{3,2,1,0:T(4,128)(2,1)} %state_hbm.1, s32[2,4,4,4,640]{4,3,2,1,0:T(4,128)} %signs_hbm.1, f32[1000,640]{1,0:T(8,128)} %time_hbm.1, f32[640]{0:T(1024)} %gain_hbm.1, f32[640]{0:T(1024)} %shift_hbm.1, f32[640]{0:T(1024)} %bias_hbm.1, ...), custom_call_target="tpu_custom_call" | custom-call | tf_op jit(solution)/shard_map/pallas_call | solution.py:378
  23.1 1.5 %shard_map.96 = (bf16[4,4,4,640]{3,2,1,0:T(4,128)(2,1)}, f32[4]{0:T(128)}) custom-call(bf16[4,4,4,640]{3,2,1,0:T(4,128)(2,1)} %get-tuple-element.4.state_ref, f32[1,128]{1,0:T(1,128)} %get-tuple-element.5.total_ref), custom_call_target="tpu_custom_call" | custom-call | tf_op jit(solution)/shard_map/pallas_call | solution.py:416
